TPU v7x, 256 devices: a whole 4x4x8 slice. The times are simulated.
256 devices in a mesh: enc: 4 (over z_lo), lab: 64 (over z_hi, y, x, core).
Axes of the slice: x: 4, y: 4, z: 8 (z_hi: 2, z_lo: 4; z = z_hi * 4 + z_lo), core: 2. Of those that a mesh axis runs over, the one named last changes fastest.
Arguments:
- embeddings: bfloat16 [131072, 768], P(('enc', 'lab')), may hold values from -6 to 6
- classifier: float32 [4096, 768], P('lab'), may hold values from -0.21875 to 0.21875
- label_valid: int32 [4096], P('lab'), may hold values 0 or 1
- shortlist: int32 [131072, 4], P(('enc', 'lab')), may hold values from 0 to 63, all different within a row; in each aligned block of 512 rows (0 to 511, 512 to 1023, ...) at most 48 rows name the same one
- slot_live: int32 [131072, 4], P(('enc', 'lab')), may hold values 0 or 1
- positive: int32 [131072, 4], P(('enc', 'lab')), may hold values from 0 to 63
- negative: int32 [131072, 4, 8], P(('enc', 'lab')), may hold values from 0 to 63
Outputs:
- w_grad: float32 [4096, 768], P('lab')
- emb_grad: float32 [131072, 768], P(('enc', 'lab'))
Inputs may be any that keep to these rules, and one draw needn't show every extreme that they name: `shortlist`: each document names 4 different clusters; among the 512 documents of one device no cluster is named by more than 48 documents.
All inputs are finite; a program needn't handle non-finite values. No bound on the sum of `label_valid` or of `slot_live` on one device may be relied on, other than what follows from the above.
Results may differ from a plain program's by a relative error of at most 0.0041.
Values may be sent and summed in bfloat16 or wider, within the bound.
A program may use at most 128 MiB of HBM per device.

v0:
```python
import math
import jax
import jax.numpy as jnp
from jax import lax
from jax.sharding import PartitionSpec as P


def dense_targets(shortlist, slot_live, positive, negative, clusters, panel):
    labels = jnp.arange(panel, dtype=jnp.int32)
    pos_hot = (positive[..., None] == labels).astype(jnp.float32)
    neg_count = jnp.sum((negative[..., None] == labels).astype(jnp.float32), axis=2)
    live = slot_live.astype(jnp.float32)[..., None]
    slot_weight = live * (pos_hot + neg_count)
    cluster_hot = (shortlist[..., None] == jnp.arange(clusters, dtype=jnp.int32)).astype(
        jnp.float32
    )
    count = shortlist.shape[0]
    weight = jnp.einsum("nsc,nsj->ncj", cluster_hot, slot_weight).reshape(count, clusters * panel)
    target = jnp.einsum("nsc,nsj->ncj", cluster_hot, pos_hot).reshape(count, clusters * panel)
    return (weight.astype(jnp.bfloat16), target.astype(jnp.bfloat16))


def make_absorb(embeddings, weight_all, target_all):

    def absorb(carry, pieces, start):
        w_piece, v_piece = pieces
        weight = weight_all.astype(jnp.float32)
        weight = weight * v_piece.astype(jnp.float32)[None, :]
        target = target_all.astype(jnp.float32)
        logits = lax.dot_general(
            embeddings, w_piece, (((1,), (1,)), ((), ())), preferred_element_type=jnp.float32
        )
        dlogits = (weight * (jax.nn.sigmoid(logits) - target)).astype(jnp.bfloat16)
        grad_acc = jnp.dot(dlogits, w_piece, preferred_element_type=jnp.float32)
        return (grad_acc, dlogits)

    return absorb


def shards(embeddings, classifier, label_valid, shortlist, slot_live, positive, negative):
    lab_count = lax.axis_size("lab")
    enc_count = lax.axis_size("enc")
    docs, width = embeddings.shape
    panel = classifier.shape[0]
    slots = shortlist.shape[1]
    classifier_b = classifier.astype(jnp.bfloat16)
    weight_all, target_all = dense_targets(
        shortlist, slot_live, positive, negative, lab_count, panel
    )
    absorb = make_absorb(embeddings, weight_all, target_all)
    initial = (
        jnp.zeros((docs, width), jnp.float32),
        jnp.zeros((docs, lab_count * panel), jnp.bfloat16),
    )
    emb_grad, scored = absorb(
        initial,
        (
            lax.all_gather(classifier_b, "lab", axis=0, tiled=True),
            lax.all_gather(label_valid.astype(jnp.bfloat16), "lab", axis=0, tiled=True),
        ),
        jnp.int32(0),
    )
    partial_grad = lax.psum_scatter(
        lax.dot_general(
            scored, embeddings, (((0,), (0,)), ((), ())), preferred_element_type=jnp.float32
        ),
        "lab",
        scatter_dimension=0,
        tiled=True,
    )
    scale_factor = 1.0 / math.sqrt(docs * enc_count * slots)
    w_grad = lax.psum(partial_grad, "enc") * scale_factor
    return (w_grad, emb_grad)


def solution(mesh):
    in_specs = (
        P(("enc", "lab"), None),
        P("lab", None),
        P("lab"),
        P(("enc", "lab"), None),
        P(("enc", "lab"), None),
        P(("enc", "lab"), None),
        P(("enc", "lab"), None, None),
    )
    out_specs = (P("lab", None), P(("enc", "lab"), None))
    return jax.shard_map(shards, mesh=mesh, in_specs=in_specs, out_specs=out_specs, check_vma=False)
```

profile of v0, /device:TPU:2, one launch (start us, length us, event | category | flops | bytes accessed | tf_op | source)
XLA Modules:
  0.0 586.9 jit_solution(4797817930439539385)
XLA Ops:
  7.2 0.0 copy-start
  7.2 0.0 all-gather.2.cloned.1.call-start
  7.2 1.6 convert_element_type.50
  8.9 0.0 all-gather.2.cloned.1.call-update
  8.9 0.0 reduce-scatter.2.cloned.1.call-start
  8.9 0.8 copy.21
  9.8 0.7 convert_element_type.42
  10.5 1.4 convert_reduce_fusion
  11.9 0.8 add_multiply_fusion
  12.7 0.3 copy.22
  13.0 8.6 %convert_convert_fusion.1 = f32[512,64,64]{2,1,0:T(8,128)} fusion(bf16[512,4,64]{2,1,0:T(4,128)(2,1)S(1)} %copy.22, s32[512,4]{1,0:T(8,128)S(1)} %copy.21), kind=kOutput, calls=%fused_computation.2 | convolution fusion | flops 19005440 | bytes 8658944 | tf_op jit(solution)/shard_map/nsc,nsj->ncj/dot_general | solution.py:18
  21.6 12.8 %copy.23 = f32[512,64,64]{0,2,1:T(8,128)} copy(f32[512,64,64]{2,1,0:T(8,128)} %convert_convert_fusion.1) | data formatting | bytes 16777216 | tf_op jit(solution)/shard_map/convert_element_type | solution.py:27
  34.4 0.0 copy-start.1
  34.4 8.9 %copy.24 = f32[512,4096]{1,0:T(8,128)} copy(f32[512,4096]{0,1:T(8,128)} %bitcast.11) | data formatting | bytes 16777216 | tf_op jit(solution)/shard_map/convert_element_type | solution.py:27
  43.3 0.0 copy-done.1
  43.4 0.1 iota_compare_fusion.4
  43.4 0.4 copy.25
  43.9 8.7 %convert_convert_fusion = f32[512,64,64]{2,1,0:T(8,128)} fusion(pred[512,4,64]{2,1,0:T(4,128)(4,1)S(1)} %copy.25, s32[512,4]{1,0:T(8,128)S(1)} %copy.21), kind=kOutput, calls=%fused_computation.1 | convolution fusion | flops 21102592 | bytes 8527872 | tf_op jit(solution)/shard_map/nsc,nsj->ncj/dot_general | solution.py:19
  52.5 12.8 %copy.26 = f32[512,64,64]{0,2,1:T(8,128)} copy(f32[512,64,64]{2,1,0:T(8,128)} %convert_convert_fusion) | data formatting | bytes 16777216 | tf_op jit(solution)/shard_map/convert_element_type | solution.py:29
  65.3 0.0 copy-start.2
  65.3 0.0 copy-start.3
  65.3 9.0 %copy.27 = f32[512,4096]{1,0:T(8,128)} copy(f32[512,4096]{0,1:T(8,128)} %bitcast.12) | data formatting | bytes 16777216 | tf_op jit(solution)/shard_map/convert_element_type | solution.py:29
  74.3 0.0 copy-done.2
  74.3 0.0 copy-done.3
  74.3 0.6 dynamic-slice
  75.5 0.2 dynamic-update-slice
  75.8 205.7 %all-reduce = bf16[4096]{0:T(1024)(128)(2,1)S(1)} all-reduce(bf16[4096]{0:T(1024)(128)(2,1)S(1)} %dynamic-update-slice), channel_id=1, replica_groups=mesh['enc'=4,'lab'=64] {'lab'}, use_global_device_ids=true, to_apply=%add | all-reduce | flops 4096 | bytes 16384
  281.5 0.0 all-gather.2.cloned.1.call-done
  281.5 0.0 copy-done
  281.6 11.0 %multiply_convert_fusion = bf16[512,4096]{1,0:T(8,128)(2,1)} fusion(f32[512,4096]{1,0:T(8,128)} %copy.27, f32[512,4096]{1,0:T(8,128)} %copy.24, bf16[512,768]{1,0:T(8,128)(2,1)S(1)} %copy-done, bf16[4096,768]{1,0:T(8,128)(2,1)} %all-gather.2.cloned.1.call-done, f32[4096]{0:T(1024)S(1)} %convert_element_type.49), kind=kOutput, calls=%fused_computation | convolution fusion | flops 3235905536 | bytes 28065792 | tf_op jit(solution)/shard_map/dot_general | solution.py:30
  292.5 10.2 %fusion.2 = f32[4096,768]{1,0:T(8,128)} fusion(bf16[512,4096]{1,0:T(8,128)(2,1)} %multiply_convert_fusion, bf16[512,768]{1,0:T(8,128)(2,1)S(1)} %copy-done), kind=kOutput, calls=%fused_computation.11 | convolution fusion | flops 3221225472 | bytes 17563648 | tf_op jit(solution)/shard_map/dot_general | solution.py:64
  302.8 0.0 reduce-scatter.2.cloned.1.call-update
  302.8 0.0 all-reduce.3.cloned.1.call-start
  302.8 228.7 %reduce-scatter.2.cloned.1.call-done = f32[64,768]{1,0:T(8,128)} async-done(((f32[4096,768]{1,0:T(8,128)}), f32[64,768]{1,0:T(8,128)}) %reduce-scatter.2.cloned.1.call-update) | async-done | bytes 196624 | tf_op jit(solution)/shard_map/reduce_scatter | solution.py:63
  531.6 0.0 all-reduce.3.cloned.1.call-update
  531.6 8.6 %fusion.3 = f32[512,768]{1,0:T(8,128)} fusion(bf16[512,4096]{1,0:T(8,128)(2,1)} %multiply_convert_fusion, bf16[4096,768]{1,0:T(8,128)(2,1)} %all-gather.2.cloned.1.call-done), kind=kOutput, calls=%fused_computation.12 | convolution fusion | flops 3221225472 | bytes 12058624 | tf_op jit(solution)/shard_map/dot_general | solution.py:34
  540.2 38.6 %all-reduce.3.cloned.1.call-done = f32[64,768]{1,0:T(8,128)} async-done(((f32[64,768]{1,0:T(8,128)}), f32[64,768]{1,0:T(8,128)}) %all-reduce.3.cloned.1.call-update) | async-done | bytes 196624 | tf_op jit(solution)/shard_map/psum | solution.py:72
  578.8 1.6 broadcast_multiply_fusion
  (3 shorter events, 0.0 us)
Async XLA Ops:
  7.2 274.4 %copy-start = (bf16[512,768]{1,0:T(8,128)(2,1)S(1)}, bf16[512,768]{1,0:T(8,128)(2,1)}, u32[]{:S(2)}) copy-start(bf16[512,768]{1,0:T(8,128)(2,1)} %param.7) | copy-start | bytes 2359300
  7.2 274.4 %all-gather.2.cloned.1.call-start = ((), (), s32[]{:S(2)}) async-start(), calls=%async_computation.1 | async-start | bytes 6389760 | tf_op jit(solution)/shard_map/all_gather | solution.py:58
  8.9 522.7 %reduce-scatter.2.cloned.1.call-start = ((), (), s32[]{:S(2)}) async-start(), calls=%async_computation.2 | async-start | bytes 12779520 | tf_op jit(solution)/shard_map/reduce_scatter | solution.py:63
  34.4 9.0 %copy-start.1 = (s32[512,4]{0,1:T(4,128)S(1)}, s32[512,4]{0,1:T(4,128)}, u32[]{:S(2)}) copy-start(s32[512,4]{0,1:T(4,128)} %param.12) | copy-start | bytes 24580
  65.3 9.0 %copy-start.2 = (s32[64]{0:T(128)S(1)}, s32[64]{0:T(128)}, u32[]{:S(2)}) copy-start(s32[64]{0:T(128)} %param.9) | copy-start | bytes 772
  65.3 9.0 %copy-start.3 = (u32[256]{0:T(256)S(1)}, u32[256]{0:T(256)}, u32[]{:S(2)}) copy-start(u32[256]{0:T(256)} %constant.8) | copy-start | bytes 3076
  302.8 276.0 %all-reduce.3.cloned.1.call-start = ((), (), s32[]{:S(2)}) async-start(), calls=%async_computation.3 | async-start | bytes 393216 | tf_op jit(solution)/shard_map/psum | solution.py:72
Sparse Core Ops, SparseCore 0:
  12.3 104.1 all-gather.1
  302.9 228.6 reduce-scatter.1
  534.2 44.5 all-reduce.2
where the time goes:
time: 588 us; the launch traced here: 587 us
  waiting for transfers between devices  267 us (45%)
  blocking collectives  206 us (35%)
  matrix products  47 us (8%)
  local copies, waits for them, and re-layouts  45.9 us (8%)
  between operations  14.5 us (2%)
  other arithmetic  6.25 us (1%)
    reduce_scatter x1, waiting for transfers between devices, shards(): lax.psum_scatter(lax.dot_general(scored, embeddings, (((0,), (0,)), ((),...  229 us
    unnamed x1, blocking collectives  206 us
    psum x1, waiting for transfers between devices, shards(): w_grad = lax.psum(partial_grad, 'enc') * scale_factor  38.6 us
    convert_element_type x2, local copies, waits for them, and re-layouts, absorb(): weight = weight_all.astype(jnp.float32)  21.8 us
    convert_element_type x2, local copies, waits for them, and re-layouts, absorb(): target = target_all.astype(jnp.float32)  21.7 us
  transfers between devices with their start and end apart: 3, of which 2 were waited for; matrix products, arithmetic and copies ran while one was open for 13% of the time, Pallas kernels for 0%

commit v1 on v0

--- a/solution.py
+++ b/solution.py
@@ -69,7 +69,12 @@
         tiled=True,
     )
     scale_factor = 1.0 / math.sqrt(docs * enc_count * slots)
-    w_grad = lax.psum(partial_grad, "enc") * scale_factor
+
+    def return_all_the_tables(my_tile):
+        arr_next = jnp.sum(lax.all_gather(my_tile, "enc"), axis=0)
+        return arr_next
+
+    w_grad = return_all_the_tables(partial_grad) * scale_factor
     return (w_grad, emb_grad)
 
 

time: 588 us -> 558 us (0.949)
  waiting for transfers between devices: 267 us -> 220 us
  blocking collectives: 206 us -> 224 us
    psum x1 -> x0, waiting for transfers between devices: 38.6 us -> none  [shards(): w_grad = lax.psum(partial_grad, 'enc') * scale_factor]
    all_gather x0 -> x1, blocking collectives: none -> 17.8 us  [return_all_the_tables(): arr_next = jnp.sum(lax.all_gather(my_tile, 'enc'), axis=0)]
    reduce_scatter x1, waiting for transfers between devices: 229 us -> 220 us  [shards(): lax.psum_scatter(lax.dot_general(scored, embeddings, (((0,), (0,)), ((),...]
  transfers between devices with their start and end apart: 3 -> 2, of which waited for: 2 -> 1; matrix products, arithmetic and copies ran while one was open for 13% -> 13% of each run, Pallas kernels for 0% -> 0%
where the time goes in v1:
time: 558 us; the launch traced here: 557 us
  blocking collectives  224 us (40%)
  waiting for transfers between devices  220 us (39%)
  matrix products  47.1 us (8%)
  local copies, waits for them, and re-layouts  45.9 us (8%)
  between operations  14.8 us (3%)
    reduce_scatter x1, waiting for transfers between devices, shards(): lax.psum_scatter(lax.dot_general(scored, embeddings, (((0,), (0,)), ((),...  220 us
    unnamed x1, blocking collectives  206 us
    convert_element_type x2, local copies, waits for them, and re-layouts, absorb(): target = target_all.astype(jnp.float32)  21.7 us
    convert_element_type x2, local copies, waits for them, and re-layouts, absorb(): weight = weight_all.astype(jnp.float32)  21.7 us
    all_gather x1, blocking collectives, return_all_the_tables(): arr_next = jnp.sum(lax.all_gather(my_tile, 'enc'), axis=0)  17.8 us
  transfers between devices with their start and end apart: 2, of which 1 were waited for; matrix products, arithmetic and copies ran while one was open for 13% of the time, Pallas kernels for 0%

profile of v1, /device:TPU:2, one launch (start us, length us, event | category | flops | bytes accessed | tf_op | source)
XLA Modules:
  0.0 557.0 jit_solution(889268817074462111)
XLA Ops:
  7.2 0.0 copy-start
  7.2 0.0 all-gather.3.cloned.1.call-start
  7.2 1.6 convert_element_type.50
  8.9 0.0 all-gather.3.cloned.1.call-update
  8.9 0.0 reduce-scatter.2.cloned.1.call-start
  8.9 0.8 copy.21
  9.8 0.7 convert_element_type.42
  10.5 1.4 convert_reduce_fusion
  11.9 0.8 add_multiply_fusion
  12.7 0.3 copy.22
  13.0 8.6 %convert_convert_fusion.1 = f32[512,64,64]{2,1,0:T(8,128)} fusion(bf16[512,4,64]{2,1,0:T(4,128)(2,1)S(1)} %copy.22, s32[512,4]{1,0:T(8,128)S(1)} %copy.21), kind=kOutput, calls=%fused_computation.2 | convolution fusion | flops 19005440 | bytes 8658944 | tf_op jit(solution)/shard_map/nsc,nsj->ncj/dot_general | solution.py:18
  21.6 12.8 %copy.23 = f32[512,64,64]{0,2,1:T(8,128)} copy(f32[512,64,64]{2,1,0:T(8,128)} %convert_convert_fusion.1) | data formatting | bytes 16777216 | tf_op jit(solution)/shard_map/convert_element_type | solution.py:27
  34.4 0.0 copy-start.1
  34.4 8.9 %copy.24 = f32[512,4096]{1,0:T(8,128)} copy(f32[512,4096]{0,1:T(8,128)} %bitcast.12) | data formatting | bytes 16777216 | tf_op jit(solution)/shard_map/convert_element_type | solution.py:27
  43.3 0.0 copy-done.1
  43.3 0.1 iota_compare_fusion.4
  43.4 0.4 copy.25
  43.9 8.7 %convert_convert_fusion = f32[512,64,64]{2,1,0:T(8,128)} fusion(pred[512,4,64]{2,1,0:T(4,128)(4,1)S(1)} %copy.25, s32[512,4]{1,0:T(8,128)S(1)} %copy.21), kind=kOutput, calls=%fused_computation.1 | convolution fusion | flops 21102592 | bytes 8527872 | tf_op jit(solution)/shard_map/nsc,nsj->ncj/dot_general | solution.py:19
  52.5 12.8 %copy.26 = f32[512,64,64]{0,2,1:T(8,128)} copy(f32[512,64,64]{2,1,0:T(8,128)} %convert_convert_fusion) | data formatting | bytes 16777216 | tf_op jit(solution)/shard_map/convert_element_type | solution.py:29
  65.3 0.0 copy-start.2
  65.3 0.0 copy-start.3
  65.3 9.0 %copy.27 = f32[512,4096]{1,0:T(8,128)} copy(f32[512,4096]{0,1:T(8,128)} %bitcast.13) | data formatting | bytes 16777216 | tf_op jit(solution)/shard_map/convert_element_type | solution.py:29
  74.3 0.0 copy-done.2
  74.3 0.0 copy-done.3
  74.3 0.6 dynamic-slice
  75.5 0.2 dynamic-update-slice
  75.8 205.7 %all-reduce = bf16[4096]{0:T(1024)(128)(2,1)S(1)} all-reduce(bf16[4096]{0:T(1024)(128)(2,1)S(1)} %dynamic-update-slice), channel_id=1, replica_groups=mesh['enc'=4,'lab'=64] {'lab'}, use_global_device_ids=true, to_apply=%add | all-reduce | flops 4096 | bytes 16384
  281.5 0.0 all-gather.3.cloned.1.call-done
  281.5 0.0 copy-done
  281.5 11.0 %multiply_convert_fusion = bf16[512,4096]{1,0:T(8,128)(2,1)} fusion(f32[512,4096]{1,0:T(8,128)} %copy.27, f32[512,4096]{1,0:T(8,128)} %copy.24, bf16[512,768]{1,0:T(8,128)(2,1)S(1)} %copy-done, bf16[4096,768]{1,0:T(8,128)(2,1)} %all-gather.3.cloned.1.call-done, f32[4096]{0:T(1024)S(1)} %convert_element_type.49), kind=kOutput, calls=%fused_computation | convolution fusion | flops 3235905536 | bytes 28065792 | tf_op jit(solution)/shard_map/dot_general | solution.py:30
  292.5 10.2 %fusion.2 = f32[4096,768]{1,0:T(8,128)} fusion(bf16[512,4096]{1,0:T(8,128)(2,1)} %multiply_convert_fusion, bf16[512,768]{1,0:T(8,128)(2,1)S(1)} %copy-done), kind=kOutput, calls=%fused_computation.11 | convolution fusion | flops 3221225472 | bytes 17563648 | tf_op jit(solution)/shard_map/dot_general | solution.py:64
  302.8 0.0 reduce-scatter.2.cloned.1.call-update
  302.8 8.6 %fusion.3 = f32[512,768]{1,0:T(8,128)} fusion(bf16[512,4096]{1,0:T(8,128)(2,1)} %multiply_convert_fusion, bf16[4096,768]{1,0:T(8,128)(2,1)} %all-gather.3.cloned.1.call-done), kind=kOutput, calls=%fused_computation.12 | convolution fusion | flops 3221225472 | bytes 12058624 | tf_op jit(solution)/shard_map/dot_general | solution.py:34
  311.4 220.2 %reduce-scatter.2.cloned.1.call-done = f32[64,768]{1,0:T(8,128)} async-done(((f32[4096,768]{1,0:T(8,128)}), f32[64,768]{1,0:T(8,128)}) %reduce-scatter.2.cloned.1.call-update) | async-done | bytes 196624 | tf_op jit(solution)/shard_map/reduce_scatter | solution.py:63
  531.6 17.8 %all-gather = f32[256,768]{1,0:T(8,128)S(1)} all-gather(f32[64,768]{1,0:T(8,128)} %reduce-scatter.2.cloned.1.call-done), channel_id=2, replica_groups=mesh['enc'=4,'lab'=64] {'enc'}, dimensions={0}, use_global_device_ids=true | all-gather | bytes 983040 | tf_op jit(solution)/shard_map/all_gather | solution.py:74
  549.5 0.7 broadcast_multiply_fusion
  (4 shorter events, 0.1 us)
Async XLA Ops:
  7.2 274.4 %copy-start = (bf16[512,768]{1,0:T(8,128)(2,1)S(1)}, bf16[512,768]{1,0:T(8,128)(2,1)}, u32[]{:S(2)}) copy-start(bf16[512,768]{1,0:T(8,128)(2,1)} %param.7) | copy-start | bytes 2359300
  7.2 274.3 %all-gather.3.cloned.1.call-start = ((), (), s32[]{:S(2)}) async-start(), calls=%async_computation.1 | async-start | bytes 6389760 | tf_op jit(solution)/shard_map/all_gather | solution.py:58
  8.9 522.7 %reduce-scatter.2.cloned.1.call-start = ((), (), s32[]{:S(2)}) async-start(), calls=%async_computation.2 | async-start | bytes 12779520 | tf_op jit(solution)/shard_map/reduce_scatter | solution.py:63
  34.4 8.9 %copy-start.1 = (s32[512,4]{0,1:T(4,128)S(1)}, s32[512,4]{0,1:T(4,128)}, u32[]{:S(2)}) copy-start(s32[512,4]{0,1:T(4,128)} %param.12) | copy-start | bytes 24580
  65.3 9.0 %copy-start.2 = (s32[64]{0:T(128)S(1)}, s32[64]{0:T(128)}, u32[]{:S(2)}) copy-start(s32[64]{0:T(128)} %param.9) | copy-start | bytes 772
  65.3 9.0 %copy-start.3 = (u32[256]{0:T(256)S(1)}, u32[256]{0:T(256)}, u32[]{:S(2)}) copy-start(u32[256]{0:T(256)} %constant.8) | copy-start | bytes 3076
Sparse Core Ops, SparseCore 0:
  12.3 104.1 all-gather.2
  302.9 228.6 reduce-scatter.1
